TPU v7x, 128 devices: a whole 4x4x4 slice. The times are simulated.
128 devices in a mesh: wide: 16 (over z_hi, x, core), narrow: 8 (over z_lo, y).
Axes of the slice: x: 4, y: 4, z: 4 (z_hi: 2, z_lo: 2; z = z_hi * 2 + z_lo), core: 2. Of those that a mesh axis runs over, the one named last changes fastest.
Arguments:
- tokens: bfloat16 [12288, 1024], P(('wide', 'narrow')), may hold values from -6 to 6
- cotangent: bfloat16 [12288, 1024], P(('wide', 'narrow')), may hold values from -6 to 6
- segments: int32 [16, 768], P('wide'), may hold values from 0 to 3, never falling along the last dimension, each value on 1 to 384 neighbouring positions
- w_query: bfloat16 [1024, 1024], P(None, 'narrow'), may hold values from -0.1875 to 0.1875
- w_key: bfloat16 [1024, 1024], P(None, 'narrow'), may hold values from -0.1875 to 0.1875
- w_value: bfloat16 [1024, 1024], P(None, 'narrow'), may hold values from -0.1875 to 0.1875
- w_out: bfloat16 [1024, 1024], P('narrow'), may hold values from -1.5 to 1.5
- w_gate: bfloat16 [1024, 4096], P(None, 'narrow'), may hold values from -0.1875 to 0.1875
- w_up: bfloat16 [1024, 4096], P(None, 'narrow'), may hold values from -0.1875 to 0.1875
- w_down: bfloat16 [4096, 1024], P('narrow'), may hold values from -0.09375 to 0.09375
- gain_one: float32 [1024], replicated, may hold values from 0.25 to 1.75
- bias_one: float32 [1024], replicated, may hold values from -2.5 to 2.5
- gain_two: float32 [1024], replicated, may hold values from 0.25 to 1.75
- bias_two: float32 [1024], replicated, may hold values from -2.5 to 2.5
Outputs:
- layer_out: float32 [12288, 1024], P(('wide', 'narrow'))
- input_grad: float32 [12288, 1024], P(('wide', 'narrow'))
- grad_query: float32 [1024, 1024], P(None, 'narrow')
- grad_key: float32 [1024, 1024], P(None, 'narrow')
- grad_value: float32 [1024, 1024], P(None, 'narrow')
- grad_out: float32 [1024, 1024], P('narrow')
- grad_gate: float32 [1024, 4096], P(None, 'narrow')
- grad_up: float32 [1024, 4096], P(None, 'narrow')
- grad_down: float32 [4096, 1024], P('narrow')
- grad_gain_one: float32 [1024], replicated
- grad_bias_one: float32 [1024], replicated
- grad_gain_two: float32 [1024], replicated
- grad_bias_two: float32 [1024], replicated
Inputs may be any that keep to these rules, and one draw needn't show every extreme that they name: `segments`: within each row of 768 tokens segment numbers never fall; each segment holds 1 to 384 tokens and one holds exactly 384.
All inputs are finite; a program needn't handle non-finite values.
Results may differ from a plain program's by a relative error of at most 0.03.
Values may be sent and summed in bfloat16 or wider, within the bound.
No kernel may reach another device: no remote copies, remote signals or barrier semaphores. Data moves between devices by JAX's collectives and lax.ppermute only.
A program may use at most 128 MiB of HBM per device.

v0:
```python
import math

import jax
import jax.numpy as jnp
from jax import lax
from jax.sharding import PartitionSpec as P

HD = 64
EPS = 1e-05
MASKED = -1e30
F32 = jnp.float32
BF16 = jnp.bfloat16


def normalize(values, gain_vec, bias_vec):
    centred = values - jnp.mean(values, axis=-1, keepdims=True)
    inverse = lax.rsqrt(jnp.mean(centred * centred, axis=-1, keepdims=True) + EPS)
    scaled = centred * inverse
    return (scaled * gain_vec + bias_vec, scaled, inverse)


def normalize_back(grad_in, scaled, inverse, gain_vec):
    along = grad_in * gain_vec
    return inverse * (
        along
        - jnp.mean(along, axis=-1, keepdims=True)
        - scaled * jnp.mean(along * scaled, axis=-1, keepdims=True)
    )


def contract_last(left_side, right_side):
    return lax.dot_general(
        left_side, right_side, (((1,), (1,)), ((), ())), preferred_element_type=F32
    )


def contract_first(left_side, right_side):
    return lax.dot_general(
        left_side, right_side, (((0,), (0,)), ((), ())), preferred_element_type=F32
    )


def rotate(values, cosine_table, sine_table):
    half_width = values.shape[-1] // 2
    first_half = values[..., :half_width]
    second_half = values[..., half_width:]
    cosine = cosine_table[:, None, :]
    sine_part = sine_table[:, None, :]
    return jnp.concatenate(
        [
            first_half * cosine - second_half * sine_part,
            second_half * cosine + first_half * sine_part,
        ],
        axis=-1,
    )


def unrotate(values, cosine_table, sine_table):
    half_width = values.shape[-1] // 2
    first_half = values[..., :half_width]
    second_half = values[..., half_width:]
    cosine = cosine_table[:, None, :]
    sine_part = sine_table[:, None, :]
    return jnp.concatenate(
        [
            first_half * cosine + second_half * sine_part,
            second_half * cosine - first_half * sine_part,
        ],
        axis=-1,
    )


def narrow_gather(own, count):
    slots = jnp.broadcast_to(own[None], (count,) + own.shape)
    got = lax.all_to_all(slots, "narrow", 0, 0, tiled=False)
    return got.reshape(count * own.shape[0], own.shape[1])


def narrow_scatter(partial, count):
    blocks = partial.reshape(count, partial.shape[0] // count, partial.shape[1])
    got = lax.all_to_all(blocks, "narrow", 0, 0, tiled=False)
    return jnp.sum(got.astype(F32), axis=0)


def narrow_gather_async(own, count):
    index = lax.axis_index("narrow")
    rows = own.shape[0]
    whole = jnp.zeros((count * rows, own.shape[1]), own.dtype)
    whole = lax.dynamic_update_slice_in_dim(whole, own, index * rows, 0)
    for k in range(1, count):
        got = lax.ppermute(own, "narrow", [((i + k) % count, i) for i in range(count)])
        whole = lax.dynamic_update_slice_in_dim(whole, got, ((index + k) % count) * rows, 0)
    return whole


def split_hi_lo(values):
    high = values.astype(BF16)
    return high, (values - high.astype(F32)).astype(BF16)


def wide_layout(wide):
    chips_x = wide // 4
    w = lax.axis_index("wide")
    return chips_x, w % 2, (w // 2) % chips_x, w // (2 * chips_x)


def wide_map(wide, dcore=0, dx=0, dz=0, flip_core=False, xor_x=0):
    chips_x = wide // 4
    pairs = []
    for v in range(wide):
        c, xx, zz = v % 2, (v // 2) % chips_x, v // (2 * chips_x)
        c2 = (1 - c) if flip_core else c
        x2 = ((xx ^ xor_x) + dx) % chips_x
        z2 = (zz + dz) % 2
        pairs.append((v, z2 * 2 * chips_x + x2 * 2 + c2))
    return pairs


def tie(value, anchor):
    if anchor is None:
        return value
    return lax.optimization_barrier((value, anchor))[0]


def wide_allreduce(grad, wide, anchors=(None,) * 6):
    chips_x, core, xpos, zhi = wide_layout(wide)
    rows, cols = grad.shape
    half = rows // 2
    quarter = half // chips_x
    eighth = quarter // 2
    grad = tie(grad, anchors[0])
    keep = lax.dynamic_slice_in_dim(grad, core * half, half, 0)
    send = lax.dynamic_slice_in_dim(grad, (1 - core) * half, half, 0)
    summed = keep.astype(F32) + lax.ppermute(send, "wide", wide_map(wide, flip_core=True)).astype(F32)
    summed = tie(summed, anchors[1])
    acc = lax.dynamic_slice_in_dim(summed, xpos * quarter, quarter, 0)
    for k in range(1, chips_x):
        piece = lax.dynamic_slice_in_dim(summed, ((xpos + k) % chips_x) * quarter, quarter, 0)
        acc = acc + lax.ppermute(piece.astype(BF16), "wide", wide_map(wide, dx=k)).astype(F32)
    acc = tie(acc, anchors[2])
    mine = lax.dynamic_slice_in_dim(acc, zhi * eighth, eighth, 0)
    other = lax.dynamic_slice_in_dim(acc, (1 - zhi) * eighth, eighth, 0)
    final = (mine + lax.ppermute(other.astype(BF16), "wide", wide_map(wide, dz=1)).astype(F32)).astype(BF16)
    final = tie(final, anchors[3])
    part = jnp.zeros((quarter, cols), BF16)
    part = lax.dynamic_update_slice_in_dim(part, final, zhi * eighth, 0)
    part = lax.dynamic_update_slice_in_dim(
        part, lax.ppermute(final, "wide", wide_map(wide, dz=1)), (1 - zhi) * eighth, 0
    )
    part = tie(part, anchors[4])
    halfrows = jnp.zeros((half, cols), BF16)
    halfrows = lax.dynamic_update_slice_in_dim(halfrows, part, xpos * quarter, 0)
    for k in range(1, chips_x):
        got = lax.ppermute(part, "wide", wide_map(wide, dx=chips_x - k))
        halfrows = lax.dynamic_update_slice_in_dim(
            halfrows, got, ((xpos + k) % chips_x) * quarter, 0
        )
    halfrows = tie(halfrows, anchors[5])
    whole = jnp.zeros((rows, cols), BF16)
    whole = lax.dynamic_update_slice_in_dim(whole, halfrows, core * half, 0)
    whole = lax.dynamic_update_slice_in_dim(
        whole, lax.ppermute(halfrows, "wide", wide_map(wide, flip_core=True)), (1 - core) * half, 0
    )
    return whole.astype(F32)


def wide_allreduce_small(values, wide):
    chips_x = wide // 4
    values = values + lax.ppermute(values, "wide", wide_map(wide, flip_core=True))
    values = values + lax.ppermute(values, "wide", wide_map(wide, xor_x=1))
    if chips_x > 2:
        values = values + lax.ppermute(values, "wide", wide_map(wide, xor_x=2))
    return values + lax.ppermute(values, "wide", wide_map(wide, dz=1))


def per_device(
    tokens,
    cotangent,
    segments,
    w_query,
    w_key,
    w_value,
    w_out,
    w_gate,
    w_up,
    w_down,
    gain_one,
    bias_one,
    gain_two,
    bias_two,
):
    count = lax.axis_size("narrow")
    wide = lax.axis_size("wide")
    block, d_model = tokens.shape
    narrow_index = lax.axis_index("narrow")
    own_rows = narrow_index * block

    seg = segments[0]
    length = seg.shape[0]
    column = lax.broadcasted_iota(jnp.int32, (length, length), 1)
    same_segment = seg[:, None] == seg[None, :]
    first_index = jnp.min(jnp.where(same_segment, column, length), axis=-1)
    position = (jnp.arange(length, dtype=jnp.int32) - first_index).astype(F32)
    inverse = 10000.0 ** (-(2.0 * jnp.arange(HD // 2).astype(F32) / HD))
    angles = position[:, None] * inverse
    cosine_table, sine_table = jnp.cos(angles), jnp.sin(angles)

    head_rows = w_out.shape[0]
    first = narrow_gather(
        jnp.concatenate([tokens, cotangent, w_out], axis=0), count
    ).reshape(count, 2 * block + head_rows, d_model)
    tok_full = first[:, :block].reshape(length, d_model)
    cot_full = first[:, block : 2 * block].reshape(length, d_model)
    w_out_full = first[:, 2 * block :]

    inputs = tok_full.astype(F32)
    normed_float, scaled_one, inverse_one = normalize(inputs, gain_one, bias_one)
    normed_one = normed_float.astype(BF16)
    own_scaled_one = lax.dynamic_slice_in_dim(scaled_one, own_rows, block, 0)
    own_inverse_one = lax.dynamic_slice_in_dim(inverse_one, own_rows, block, 0)

    heads = w_query.shape[1] // HD
    head_shape = (length, heads, HD)
    queries = rotate(
        jnp.dot(normed_one, w_query, preferred_element_type=F32).reshape(head_shape),
        cosine_table,
        sine_table,
    ).astype(BF16)
    key_rows = rotate(
        jnp.dot(normed_one, w_key, preferred_element_type=F32).reshape(head_shape),
        cosine_table,
        sine_table,
    ).astype(BF16)
    value_rows = (
        jnp.dot(normed_one, w_value, preferred_element_type=F32).astype(BF16).reshape(head_shape)
    )
    score_scale = 1.0 / math.sqrt(HD)
    scores = (
        jnp.einsum("qhd,khd->hqk", queries, key_rows, preferred_element_type=F32) * score_scale
    )
    scores = jnp.where(same_segment[None], scores, MASKED)
    row_peak = jnp.max(scores, axis=-1, keepdims=True)
    exponent = jnp.exp(scores - row_peak)
    row_total = jnp.sum(exponent, axis=-1, keepdims=True)
    probs = exponent / row_total
    probs_low = probs.astype(BF16)
    attended = (
        jnp.einsum("hqk,khd->qhd", probs_low, value_rows, preferred_element_type=F32)
        .astype(BF16)
        .reshape(length, -1)
    )

    attended_all = lax.all_to_all(
        jnp.broadcast_to(attended[None], (count,) + attended.shape), "narrow", 0, 0, tiled=False
    )
    branch = jnp.einsum(
        "jtc,jcd->td", attended_all, w_out_full, preferred_element_type=F32
    )
    middle = inputs + branch
    normed_two_float, scaled_two, inverse_two = normalize(middle, gain_two, bias_two)
    normed_two = normed_two_float.astype(BF16)

    gate_pre = jnp.dot(normed_two, w_gate, preferred_element_type=F32)
    up_pre = jnp.dot(normed_two, w_up, preferred_element_type=F32)
    sigmoid_gate = jax.nn.sigmoid(gate_pre)
    active = gate_pre * sigmoid_gate
    hidden = (active * up_pre).astype(BF16)
    ffn_partial = jnp.dot(hidden, w_down, preferred_element_type=F32).astype(BF16)

    hidden_grad = contract_last(cot_full, w_down)
    gate_grad = (
        hidden_grad * up_pre * sigmoid_gate * (1.0 + gate_pre * (1.0 - sigmoid_gate))
    ).astype(BF16)
    up_grad = (hidden_grad * active).astype(BF16)
    ffn_grads = jnp.concatenate(
        [
            contract_first(normed_two, jnp.concatenate([gate_grad, up_grad], axis=1)),
            contract_first(hidden, cot_full),
        ],
        axis=0,
    ).astype(BF16)
    two_partial = (contract_last(gate_grad, w_gate) + contract_last(up_grad, w_up)).astype(BF16)
    both = narrow_scatter(jnp.concatenate([ffn_partial, two_partial], axis=1), count)
    layer_out = lax.dynamic_slice_in_dim(middle, own_rows, block, 0) + both[:, :d_model]
    own_two_grad = both[:, d_model:]
    own_scaled_two = lax.dynamic_slice_in_dim(scaled_two, own_rows, block, 0)
    own_inverse_two = lax.dynamic_slice_in_dim(inverse_two, own_rows, block, 0)

    middle_grad = cotangent.astype(F32) + normalize_back(
        own_two_grad, own_scaled_two, own_inverse_two, gain_two
    )
    branch_grad = narrow_gather(middle_grad.astype(BF16), count)

    attended_grad = contract_last(branch_grad, w_out).astype(BF16).reshape(head_shape)
    prob_grad = jnp.einsum(
        "qhd,khd->hqk", attended_grad, value_rows, preferred_element_type=F32
    )
    score_grad = (
        probs * (prob_grad - jnp.sum(probs * prob_grad, axis=-1, keepdims=True))
    ).astype(BF16)
    query_grad = score_scale * jnp.einsum(
        "hqk,khd->qhd", score_grad, key_rows, preferred_element_type=F32
    )
    key_grad = score_scale * jnp.einsum(
        "hqk,qhd->khd", score_grad, queries, preferred_element_type=F32
    )
    value_grad = jnp.einsum(
        "hqk,qhd->khd", probs_low, attended_grad, preferred_element_type=F32
    ).astype(BF16).reshape(length, -1)
    query_grad = unrotate(query_grad, cosine_table, sine_table).astype(BF16).reshape(length, -1)
    key_grad = unrotate(key_grad, cosine_table, sine_table).astype(BF16).reshape(length, -1)
    projection_grads = jnp.concatenate([query_grad, key_grad, value_grad], axis=1)
    projections = w_query.shape[1]
    qkv_grads = contract_first(normed_one, projection_grads).astype(BF16)
    attn_grads = jnp.concatenate(
        [qkv_grads, contract_first(branch_grad, attended).astype(BF16)], axis=1
    )
    one_float = contract_last(
        projection_grads, jnp.concatenate([w_query, w_key, w_value], axis=1)
    )
    norm_one = jnp.stack(
        [jnp.sum(one_float * scaled_one, axis=0), jnp.sum(one_float, axis=0)]
    )
    norm_two = jnp.stack(
        [jnp.sum(own_two_grad * own_scaled_two, axis=0), jnp.sum(own_two_grad, axis=0)]
    )
    norm_parts = jnp.concatenate([norm_one, norm_two], axis=0)
    high, low = split_hi_lo(norm_parts)
    extra = jnp.concatenate([high, low, jnp.zeros((8, d_model), BF16)], axis=0)
    one_blocks = one_float.astype(BF16).reshape(count, block, d_model)
    payload = jnp.concatenate(
        [one_blocks, jnp.broadcast_to(extra[None], (count,) + extra.shape)], axis=1
    )
    got = lax.all_to_all(payload, "narrow", 0, 0, tiled=False).astype(F32)
    summed = jnp.sum(got, axis=0)
    ffn_total = wide_allreduce(
        ffn_grads, wide, (None, both, branch_grad, projection_grads, one_float, got)
    )
    attn_total = wide_allreduce(attn_grads, wide)
    own_one_grad = summed[:block]
    norm_narrow = summed[block : block + 4] + summed[block + 4 : block + 8]
    norm_total = wide_allreduce_small(norm_narrow, wide)
    input_grad = middle_grad + normalize_back(
        own_one_grad, own_scaled_one, own_inverse_one, gain_one
    )
    ff_cols = w_gate.shape[1]
    return (
        layer_out,
        input_grad,
        attn_total[:, :projections],
        attn_total[:, projections : 2 * projections],
        attn_total[:, 2 * projections : 3 * projections],
        attn_total[:, 3 * projections :].T,
        ffn_total[:d_model, :ff_cols],
        ffn_total[:d_model, ff_cols:],
        ffn_total[d_model:],
        norm_total[0],
        norm_total[1],
        norm_total[2],
        norm_total[3],
    )


def solution(mesh):
    placed = (
        P(("wide", "narrow"), None),
        P(("wide", "narrow"), None),
        P("wide", None),
        P(None, "narrow"),
        P(None, "narrow"),
        P(None, "narrow"),
        P("narrow", None),
        P(None, "narrow"),
        P(None, "narrow"),
        P("narrow", None),
        P(),
        P(),
        P(),
        P(),
    )
    return jax.shard_map(
        per_device,
        mesh=mesh,
        in_specs=placed,
        out_specs=(
            P(("wide", "narrow"), None),
            P(("wide", "narrow"), None),
            P(None, "narrow"),
            P(None, "narrow"),
            P(None, "narrow"),
            P("narrow", None),
            P(None, "narrow"),
            P(None, "narrow"),
            P("narrow", None),
            P(),
            P(),
            P(),
            P(),
        ),
        check_vma=False,
    )
```

profile of v0, /device:TPU:16, one launch (start us, length us, event | category | flops | bytes accessed | tf_op | source)
XLA Modules:
  0.0 377.6 jit_solution(2239414128775722689)
XLA Ops:
  5.0 6.3 %all-to-all-start = ((bf16[8,320,1024]{2,1,0:T(8,128)(2,1)}), bf16[8,320,1024]{2,1,0:T(8,128)(2,1)}, u32[]{:S(2)}, u32[]{:S(2)}) async-start(bf16[8,320,1024]{2,1,0:T(8,128)(2,1)} %broadcast_in_dim.40), calls=%async_computation | async-start | bytes 10485760 | tf_op jit(solution)/shard_map/all_to_all | solution.py:75
  12.9 66.3 %all-to-all-done = bf16[8,320,1024]{2,1,0:T(8,128)(2,1)} async-done(((bf16[8,320,1024]{2,1,0:T(8,128)(2,1)}), bf16[8,320,1024]{2,1,0:T(8,128)(2,1)}, u32[]{:S(2)}, u32[]{:S(2)}) %all-to-all-start) | async-done | bytes 5242912 | tf_op jit(solution)/shard_map/all_to_all | solution.py:75
  90.0 4.0 %fusion.64 = (f32[2,768]{1,0:T(2,128)S(1)}, f32[2,768,768]{1,2,0:T(8,128)}) fusion(pred[768,768]{0,1:T(8,128)(4,1)S(1)} %broadcast_compare_fusion, bf16[768,2,32]{0,2,1:T(8,128)(2,1)S(1)} %get-tuple-element.89, bf16[768,2,32]{0,2,1:T(8,128)(2,1)S(1)} %get-tuple-element.90, bf16[768,2,32]{0,2,1:T(8,128)(2,1)S(1)} %get-tuple-element.84, ...), kind=kOutput, calls=%fused_computation.166 | convolution fusion | flops 156500736 | bytes 5707776 | tf_op jit(solution)/shard_map/sub | solution.py:243
  98.5 14.6 %all-to-all-start.1 = ((bf16[8,768,128]{2,1,0:T(8,128)(2,1)}), bf16[8,768,128]{2,1,0:T(8,128)(2,1)S(1)}, u32[]{:S(2)}, u32[]{:S(2)}) async-start(bf16[8,768,128]{2,1,0:T(8,128)(2,1)} %broadcast_in_dim.45), calls=%async_computation.1 | async-start | bytes 3145728 | tf_op jit(solution)/shard_map/all_to_all | solution.py:253
  113.1 3.5 fusion.60
  119.9 10.6 %all-to-all-done.1 = bf16[8,768,128]{2,1,0:T(8,128)(2,1)S(1)} async-done(((bf16[8,768,128]{2,1,0:T(8,128)(2,1)}), bf16[8,768,128]{2,1,0:T(8,128)(2,1)S(1)}, u32[]{:S(2)}, u32[]{:S(2)}) %all-to-all-start.1) | async-done | bytes 1572896 | tf_op jit(solution)/shard_map/all_to_all | solution.py:253
  130.5 3.9 %fusion.65 = (f32[768]{0:T(1024)S(1)}, f32[768,1024]{1,0:T(8,128)S(1)}) fusion(bf16[8,768,128]{2,1,0:T(8,128)(2,1)S(1)} %all-to-all-done.1, bf16[8,320,1024]{2,1,0:T(8,128)(2,1)} %all-to-all-done, bf16[8,96,1024]{2,1,0:T(8,128)(2,1)} %get-tuple-element.62), kind=kOutput, calls=%fused_computation.167 | convolution fusion | flops 1612971264 | bytes 8391680 | tf_op jit(solution)/shard_map/jtc,jcd->td/dot_general | solution.py:256
  146.9 7.4 %all-to-all-start.2 = ((bf16[8,96,2048]{2,1,0:T(8,128)(2,1)}), bf16[8,96,2048]{2,1,0:T(8,128)(2,1)}, u32[]{:S(2)}, u32[]{:S(2)}) async-start(bf16[8,96,2048]{2,1,0:T(8,128)(2,1)} %bitcast.81), calls=%async_computation.2 | async-start | bytes 6291456 | tf_op jit(solution)/shard_map/all_to_all | solution.py:81
  161.6 31.2 %all-to-all-done.2 = bf16[8,96,2048]{2,1,0:T(8,128)(2,1)} async-done(((bf16[8,96,2048]{2,1,0:T(8,128)(2,1)}), bf16[8,96,2048]{2,1,0:T(8,128)(2,1)}, u32[]{:S(2)}, u32[]{:S(2)}) %all-to-all-start.2) | async-done | bytes 3145760 | tf_op jit(solution)/shard_map/all_to_all | solution.py:81
  200.1 12.3 %all-to-all-start.3 = ((bf16[8,96,1024]{2,1,0:T(8,128)(2,1)}), bf16[8,96,1024]{2,1,0:T(8,128)(2,1)S(1)}, u32[]{:S(2)}, u32[]{:S(2)}) async-start(bf16[8,96,1024]{2,1,0:T(8,128)(2,1)} %broadcast_in_dim.46), calls=%async_computation.3 | async-start | bytes 3145728 | tf_op jit(solution)/shard_map/all_to_all | solution.py:75
  212.4 3.3 convert_add_fusion
  223.7 6.1 %collective-permute-done.11 = bf16[192,1024]{1,0:T(8,128)(2,1)S(1)} collective-permute-done((bf16[192,1024]{1,0:T(8,128)(2,1)S(1)}, bf16[192,1024]{1,0:T(8,128)(2,1)S(1)}, u32[]{:S(2)}, u32[]{:S(2)}) %collective-permute-start.11) | collective-permute-done | bytes 393248 | tf_op jit(solution)/shard_map/ppermute | solution.py:139
  229.9 7.3 %collective-permute-done.12 = bf16[192,1024]{1,0:T(8,128)(2,1)} collective-permute-done((bf16[192,1024]{1,0:T(8,128)(2,1)S(1)}, bf16[192,1024]{1,0:T(8,128)(2,1)}, u32[]{:S(2)}, u32[]{:S(2)}) %collective-permute-start.12) | collective-permute-done | bytes 393248 | tf_op jit(solution)/shard_map/ppermute | solution.py:139
  240.3 3.3 multiply_reduce_fusion
  254.7 5.7 %all-to-all-start.4 = ((bf16[8,112,1024]{2,1,0:T(8,128)(2,1)}), bf16[8,112,1024]{2,1,0:T(8,128)(2,1)S(1)}, u32[]{:S(2)}, u32[]{:S(2)}) async-start(bf16[8,112,1024]{2,1,0:T(8,128)(2,1)} %pad_maximum_fusion.1), calls=%async_computation.4 | async-start | bytes 3670016 | tf_op jit(solution)/shard_map/all_to_all | solution.py:334
  261.5 3.7 collective-permute-start.14
  271.9 16.6 %collective-permute-done.14 = bf16[96,1024]{1,0:T(8,128)(2,1)S(1)} collective-permute-done((bf16[96,1024]{1,0:T(8,128)(2,1)S(1)}, bf16[96,1024]{1,0:T(8,128)(2,1)S(1)}, u32[]{:S(2)}, u32[]{:S(2)}) %collective-permute-start.14) | collective-permute-done | bytes 196640 | tf_op jit(solution)/shard_map/ppermute | solution.py:143
  288.9 3.6 collective-permute-start.4
  292.6 7.3 %collective-permute-done.4 = bf16[64,512]{0,1:T(8,128)(2,1)S(1)} collective-permute-done((bf16[64,512]{0,1:T(8,128)(2,1)S(1)}, bf16[64,512]{0,1:T(8,128)(2,1)S(1)}, u32[]{:S(2)}, u32[]{:S(2)}) %collective-permute-start.4) | collective-permute-done | bytes 65568 | tf_op jit(solution)/shard_map/ppermute | solution.py:143
  313.5 11.0 %collective-permute-done.6 = bf16[128,512]{0,1:T(8,128)(2,1)S(1)} collective-permute-done((bf16[128,512]{0,1:T(8,128)(2,1)S(1)}, bf16[128,512]{0,1:T(8,128)(2,1)S(1)}, u32[]{:S(2)}, u32[]{:S(2)}) %collective-permute-start.6) | collective-permute-done | bytes 131104 | tf_op jit(solution)/shard_map/ppermute | solution.py:154
  325.5 5.7 %collective-permute-done.8 = bf16[128,512]{0,1:T(8,128)(2,1)S(1)} collective-permute-done((bf16[128,512]{0,1:T(8,128)(2,1)S(1)}, bf16[128,512]{0,1:T(8,128)(2,1)S(1)}, u32[]{:S(2)}, u32[]{:S(2)}) %collective-permute-start.8) | collective-permute-done | bytes 131104 | tf_op jit(solution)/shard_map/ppermute | solution.py:154
  352.6 3.7 collective-permute-done.21
  357.7 3.8 collective-permute-done.22
  370.1 4.2 %fusion.61 = (f32[1024,512]{1,0:T(8,128)}, f32[1024,512]{1,0:T(8,128)}) fusion(bf16[1536,1024]{1,0:T(8,128)(2,1)} %constant_dynamic-update-slice_fusion), kind=kLoop, calls=%fused_computation.163 | loop fusion | bytes 8388608 | tf_op jit(solution)/shard_map/slice | solution.py:355
  (258 shorter events, 129.9 us)
Async XLA Ops:
  5.0 74.2 %all-to-all-start = ((bf16[8,320,1024]{2,1,0:T(8,128)(2,1)}), bf16[8,320,1024]{2,1,0:T(8,128)(2,1)}, u32[]{:S(2)}, u32[]{:S(2)}) async-start(bf16[8,320,1024]{2,1,0:T(8,128)(2,1)} %broadcast_in_dim.40), calls=%async_computation | async-start | bytes 10485760 | tf_op jit(solution)/shard_map/all_to_all | solution.py:75
  98.5 31.9 %all-to-all-start.1 = ((bf16[8,768,128]{2,1,0:T(8,128)(2,1)}), bf16[8,768,128]{2,1,0:T(8,128)(2,1)S(1)}, u32[]{:S(2)}, u32[]{:S(2)}) async-start(bf16[8,768,128]{2,1,0:T(8,128)(2,1)} %broadcast_in_dim.45), calls=%async_computation.1 | async-start | bytes 3145728 | tf_op jit(solution)/shard_map/all_to_all | solution.py:253
  146.9 45.9 %all-to-all-start.2 = ((bf16[8,96,2048]{2,1,0:T(8,128)(2,1)}), bf16[8,96,2048]{2,1,0:T(8,128)(2,1)}, u32[]{:S(2)}, u32[]{:S(2)}) async-start(bf16[8,96,2048]{2,1,0:T(8,128)(2,1)} %bitcast.81), calls=%async_computation.2 | async-start | bytes 6291456 | tf_op jit(solution)/shard_map/all_to_all | solution.py:81
  161.5 50.9 %collective-permute-start.10 = (bf16[768,1024]{1,0:T(8,128)(2,1)}, bf16[768,1024]{1,0:T(8,128)(2,1)}, u32[]{:S(2)}, u32[]{:S(2)}) collective-permute-start(bf16[768,1024]{1,0:T(8,128)(2,1)} %fusion.16), channel_id=1, source_target_pairs={{0,8},{8,0},{16,24},{24,16},{32,40},{40,32},{48,56},{56,48},{64,72... | collective-permute-start | bytes 4718600 | tf_op jit(solution)/shard_map/ppermute | solution.py:134
  200.1 39.6 %all-to-all-start.3 = ((bf16[8,96,1024]{2,1,0:T(8,128)(2,1)}), bf16[8,96,1024]{2,1,0:T(8,128)(2,1)S(1)}, u32[]{:S(2)}, u32[]{:S(2)}) async-start(bf16[8,96,1024]{2,1,0:T(8,128)(2,1)} %broadcast_in_dim.46), calls=%async_computation.3 | async-start | bytes 3145728 | tf_op jit(solution)/shard_map/all_to_all | solution.py:75
  217.5 12.3 %collective-permute-start.11 = (bf16[192,1024]{1,0:T(8,128)(2,1)S(1)}, bf16[192,1024]{1,0:T(8,128)(2,1)S(1)}, u32[]{:S(2)}, u32[]{:S(2)}) collective-permute-start(bf16[192,1024]{1,0:T(8,128)(2,1)S(1)} %get-tuple-element.65), channel_id=1, source_target_pairs={{0,16},{8,24},{16,32},{24,40},{32,48},{40,56},{48,0},{56,8},{64,80... | collective-permute-start | bytes 1179656 | tf_op jit(solution)/shard_map/ppermute | solution.py:139
  219.1 18.1 %collective-permute-start.12 = (bf16[192,1024]{1,0:T(8,128)(2,1)S(1)}, bf16[192,1024]{1,0:T(8,128)(2,1)}, u32[]{:S(2)}, u32[]{:S(2)}) collective-permute-start(bf16[192,1024]{1,0:T(8,128)(2,1)S(1)} %get-tuple-element.67), channel_id=1, source_target_pairs={{0,32},{8,40},{16,48},{24,56},{32,0},{40,8},{48,16},{56,24},{64,96... | collective-permute-start | bytes 1179656 | tf_op jit(solution)/shard_map/ppermute | solution.py:139
  221.8 15.3 %collective-permute-start.13 = (bf16[192,1024]{1,0:T(8,128)(2,1)S(1)}, bf16[192,1024]{1,0:T(8,128)(2,1)}, u32[]{:S(2)}, u32[]{:S(2)}) collective-permute-start(bf16[192,1024]{1,0:T(8,128)(2,1)S(1)} %get-tuple-element.66), channel_id=1, source_target_pairs={{0,48},{8,56},{16,0},{24,8},{32,16},{40,24},{48,32},{56,40},{64,11... | collective-permute-start | bytes 1179656 | tf_op jit(solution)/shard_map/ppermute | solution.py:139
  250.2 15.0 %collective-permute-start = (bf16[512,512]{0,1:T(8,128)(2,1)S(1)}, bf16[512,512]{0,1:T(8,128)(2,1)}, u32[]{:S(2)}, u32[]{:S(2)}) collective-permute-start(bf16[512,512]{0,1:T(8,128)(2,1)S(1)} %fusion.42), channel_id=1, source_target_pairs={{0,8},{8,0},{16,24},{24,16},{32,40},{40,32},{48,56},{56,48},{64,72... | collective-permute-start | bytes 1572872 | tf_op jit(solution)/shard_map/ppermute | solution.py:134
  254.7 96.1 %all-to-all-start.4 = ((bf16[8,112,1024]{2,1,0:T(8,128)(2,1)}), bf16[8,112,1024]{2,1,0:T(8,128)(2,1)S(1)}, u32[]{:S(2)}, u32[]{:S(2)}) async-start(bf16[8,112,1024]{2,1,0:T(8,128)(2,1)} %pad_maximum_fusion.1), calls=%async_computation.4 | async-start | bytes 3670016 | tf_op jit(solution)/shard_map/all_to_all | solution.py:334
  261.5 27.0 %collective-permute-start.14 = (bf16[96,1024]{1,0:T(8,128)(2,1)S(1)}, bf16[96,1024]{1,0:T(8,128)(2,1)S(1)}, u32[]{:S(2)}, u32[]{:S(2)}) collective-permute-start(bf16[96,1024]{1,0:T(8,128)(2,1)S(1)} %dynamic-slice_convert_fusion.3), channel_id=1, source_target_pairs={{0,64},{8,72},{16,80},{24,88},{32,96},{40,104},{48,112},{56,120},{... | collective-permute-start | bytes 589832 | tf_op jit(solution)/shard_map/ppermute | solution.py:143
  266.5 22.2 %collective-permute-start.1 = (bf16[128,512]{0,1:T(8,128)(2,1)S(1)}, bf16[128,512]{0,1:T(8,128)(2,1)S(1)}, u32[]{:S(2)}, u32[]{:S(2)}) collective-permute-start(bf16[128,512]{0,1:T(8,128)(2,1)S(1)} %get-tuple-element.75), channel_id=1, source_target_pairs={{0,16},{8,24},{16,32},{24,40},{32,48},{40,56},{48,0},{56,8},{64,80... | collective-permute-start | bytes 393224 | tf_op jit(solution)/shard_map/ppermute | solution.py:139
  268.2 20.5 %collective-permute-start.2 = (bf16[128,512]{0,1:T(8,128)(2,1)S(1)}, bf16[128,512]{0,1:T(8,128)(2,1)S(1)}, u32[]{:S(2)}, u32[]{:S(2)}) collective-permute-start(bf16[128,512]{0,1:T(8,128)(2,1)S(1)} %get-tuple-element.77), channel_id=1, source_target_pairs={{0,32},{8,40},{16,48},{24,56},{32,0},{40,8},{48,16},{56,24},{64,96... | collective-permute-start | bytes 393224 | tf_op jit(solution)/shard_map/ppermute | solution.py:139
  270.3 18.4 %collective-permute-start.3 = (bf16[128,512]{0,1:T(8,128)(2,1)S(1)}, bf16[128,512]{0,1:T(8,128)(2,1)S(1)}, u32[]{:S(2)}, u32[]{:S(2)}) collective-permute-start(bf16[128,512]{0,1:T(8,128)(2,1)S(1)} %get-tuple-element.76), channel_id=1, source_target_pairs={{0,48},{8,56},{16,0},{24,8},{32,16},{40,24},{48,32},{56,40},{64,11... | collective-permute-start | bytes 393224 | tf_op jit(solution)/shard_map/ppermute | solution.py:139
  288.6 11.7 %collective-permute-start.15 = (bf16[96,1024]{1,0:T(8,128)(2,1)S(1)}, bf16[96,1024]{1,0:T(8,128)(2,1)S(1)}, u32[]{:S(2)}, u32[]{:S(2)}) collective-permute-start(bf16[96,1024]{1,0:T(8,128)(2,1)S(1)} %add_convert_fusion.5), channel_id=1, source_target_pairs={{0,64},{8,72},{16,80},{24,88},{32,96},{40,104},{48,112},{56,120},{... | collective-permute-start | bytes 589832 | tf_op jit(solution)/shard_map/ppermute | solution.py:148
  288.9 10.9 %collective-permute-start.4 = (bf16[64,512]{0,1:T(8,128)(2,1)S(1)}, bf16[64,512]{0,1:T(8,128)(2,1)S(1)}, u32[]{:S(2)}, u32[]{:S(2)}) collective-permute-start(bf16[64,512]{0,1:T(8,128)(2,1)S(1)} %dynamic-slice_convert_fusion.4), channel_id=1, source_target_pairs={{0,64},{8,72},{16,80},{24,88},{32,96},{40,104},{48,112},{56,120},{... | collective-permute-start | bytes 196616 | tf_op jit(solution)/shard_map/ppermute | solution.py:143
  300.4 30.9 %collective-permute-start.16 = (bf16[192,1024]{1,0:T(8,128)(2,1)S(1)}, bf16[192,1024]{1,0:T(8,128)(2,1)}, u32[]{:S(2)}, u32[]{:S(2)}) collective-permute-start(bf16[192,1024]{1,0:T(8,128)(2,1)S(1)} %constant_dynamic-update-slice_fusion.6), channel_id=1, source_target_pairs={{0,48},{8,56},{16,0},{24,8},{32,16},{40,24},{48,32},{56,40},{64,11... | collective-permute-start | bytes 1179656 | tf_op jit(solution)/shard_map/ppermute | solution.py:154
  302.7 30.4 %collective-permute-start.17 = (bf16[192,1024]{1,0:T(8,128)(2,1)S(1)}, bf16[192,1024]{1,0:T(8,128)(2,1)}, u32[]{:S(2)}, u32[]{:S(2)}) collective-permute-start(bf16[192,1024]{1,0:T(8,128)(2,1)S(1)} %constant_dynamic-update-slice_fusion.6), channel_id=1, source_target_pairs={{0,32},{8,40},{16,48},{24,56},{32,0},{40,8},{48,16},{56,24},{64,96... | collective-permute-start | bytes 1179656 | tf_op jit(solution)/shard_map/ppermute | solution.py:154
  304.1 30.8 %collective-permute-start.18 = (bf16[192,1024]{1,0:T(8,128)(2,1)S(1)}, bf16[192,1024]{1,0:T(8,128)(2,1)S(1)}, u32[]{:S(2)}, u32[]{:S(2)}) collective-permute-start(bf16[192,1024]{1,0:T(8,128)(2,1)S(1)} %constant_dynamic-update-slice_fusion.6), channel_id=1, source_target_pairs={{0,16},{8,24},{16,32},{24,40},{32,48},{40,56},{48,0},{56,8},{64,80... | collective-permute-start | bytes 1179656 | tf_op jit(solution)/shard_map/ppermute | solution.py:154
  307.3 17.2 %collective-permute-start.6 = (bf16[128,512]{0,1:T(8,128)(2,1)S(1)}, bf16[128,512]{0,1:T(8,128)(2,1)S(1)}, u32[]{:S(2)}, u32[]{:S(2)}) collective-permute-start(bf16[128,512]{0,1:T(8,128)(2,1)S(1)} %dynamic_update_slice.49), channel_id=1, source_target_pairs={{0,48},{8,56},{16,0},{24,8},{32,16},{40,24},{48,32},{56,40},{64,11... | collective-permute-start | bytes 393224 | tf_op jit(solution)/shard_map/ppermute | solution.py:154
  311.8 13.7 %collective-permute-start.7 = (bf16[128,512]{0,1:T(8,128)(2,1)S(1)}, bf16[128,512]{0,1:T(8,128)(2,1)S(1)}, u32[]{:S(2)}, u32[]{:S(2)}) collective-permute-start(bf16[128,512]{0,1:T(8,128)(2,1)S(1)} %dynamic_update_slice.49), channel_id=1, source_target_pairs={{0,32},{8,40},{16,48},{24,56},{32,0},{40,8},{48,16},{56,24},{64,96... | collective-permute-start | bytes 393224 | tf_op jit(solution)/shard_map/ppermute | solution.py:154
  324.5 6.6 %collective-permute-start.8 = (bf16[128,512]{0,1:T(8,128)(2,1)S(1)}, bf16[128,512]{0,1:T(8,128)(2,1)S(1)}, u32[]{:S(2)}, u32[]{:S(2)}) collective-permute-start(bf16[128,512]{0,1:T(8,128)(2,1)S(1)} %dynamic_update_slice.49), channel_id=1, source_target_pairs={{0,16},{8,24},{16,32},{24,40},{32,48},{40,56},{48,0},{56,8},{64,80... | collective-permute-start | bytes 393224 | tf_op jit(solution)/shard_map/ppermute | solution.py:154
  331.2 9.9 %collective-permute-start.9 = (bf16[512,512]{0,1:T(8,128)(2,1)S(1)}, bf16[512,512]{0,1:T(8,128)(2,1)S(1)}, u32[]{:S(2)}, u32[]{:S(2)}) collective-permute-start(bf16[512,512]{0,1:T(8,128)(2,1)S(1)} %constant_dynamic-update-slice_fusion.10), channel_id=1, source_target_pairs={{0,8},{8,0},{16,24},{24,16},{32,40},{40,32},{48,56},{56,48},{64,72... | collective-permute-start | bytes 1572872 | tf_op jit(solution)/shard_map/ppermute | solution.py:162
  335.6 31.8 %collective-permute-start.19 = (bf16[768,1024]{1,0:T(8,128)(2,1)}, bf16[768,1024]{1,0:T(8,128)(2,1)}, u32[]{:S(2)}, u32[]{:S(2)}) collective-permute-start(bf16[768,1024]{1,0:T(8,128)(2,1)} %constant_dynamic-update-slice_fusion.2), channel_id=1, source_target_pairs={{0,8},{8,0},{16,24},{24,16},{32,40},{40,32},{48,56},{56,48},{64,72... | collective-permute-start | bytes 4718600 | tf_op jit(solution)/shard_map/ppermute | solution.py:162
  (56 other events, 615.6 us)
where the time goes:
time: 385 us; the launch traced here: 378 us
  waiting for transfers between devices  172 us (45%)
  starting transfers between devices  78.9 us (20%)
  local copies, waits for them, and re-layouts  50.9 us (13%)
  other arithmetic  38.3 us (10%)
  matrix products  35 us (9%)
    all_to_all x2, waiting for transfers between devices, narrow_gather(): got = lax.all_to_all(slots, 'narrow', 0, 0, tiled=False)  66.3 us
    all_to_all x1, waiting for transfers between devices, narrow_scatter(): got = lax.all_to_all(blocks, 'narrow', 0, 0, tiled=False)  31.2 us
    ppermute x2, waiting for transfers between devices, wide_allreduce(): lax.ppermute(other.astype(BF16), 'wide', wide_map(wide, dz=1)).astype(F32)  23.9 us
    all_to_all x2, starting transfers between devices, narrow_gather(): got = lax.all_to_all(slots, 'narrow', 0, 0, tiled=False)  18.6 us
    ppermute x6, waiting for transfers between devices, wide_allreduce(): got = lax.ppermute(part, 'wide', wide_map(wide, dx=chips_x - k))  17.4 us
    all_to_all x1, starting transfers between devices, per_device(): lax.all_to_all(jnp.broadcast_to(attended[None], (count,) + attended.shape...  14.6 us
    ppermute x6, waiting for transfers between devices, wide_allreduce(): lax.ppermute(piece.astype(BF16), 'wide', wide_map(wide, dx=k)).astype(F32)  13.4 us
    unnamed x107, local copies, waits for them, and re-layouts  13.3 us
  transfers between devices with their start and end apart: 29, of which 14 were waited for; matrix products, arithmetic and copies ran while one was open for 16% of the time, Pallas kernels for 0%

commit v1 on v0

--- a/solution.py
+++ b/solution.py
@@ -333,10 +333,8 @@
     )
     got = lax.all_to_all(payload, "narrow", 0, 0, tiled=False).astype(F32)
     summed = jnp.sum(got, axis=0)
-    ffn_total = wide_allreduce(
-        ffn_grads, wide, (None, both, branch_grad, projection_grads, one_float, got)
-    )
-    attn_total = wide_allreduce(attn_grads, wide)
+    attn_total = wide_allreduce(attn_grads, wide, (None, payload, None, None, None, None))
+    ffn_total = tie(lax.psum(ffn_grads, "wide"), got).astype(F32)
     own_one_grad = summed[:block]
     norm_narrow = summed[block : block + 4] + summed[block + 4 : block + 8]
     norm_total = wide_allreduce_small(norm_narrow, wide)

time: 385 us -> 431 us (1.12)
  the two profiles are of different devices: /device:TPU:16 before, /device:TPU:0 now
where the time goes in v1:
time: 431 us; the launch traced here: 424 us
  waiting for transfers between devices  236 us (55%)
  starting transfers between devices  72.5 us (17%)
  matrix products  35.5 us (8%)
  local copies, waits for them, and re-layouts  33.8 us (8%)
  other arithmetic  30.6 us (7%)
  between operations  15.2 us (4%)
    psum x1, waiting for transfers between devices, per_device(): ffn_total = tie(lax.psum(ffn_grads, 'wide'), got).astype(F32)  84.1 us
    all_to_all x2, waiting for transfers between devices, narrow_gather(): got = lax.all_to_all(slots, 'narrow', 0, 0, tiled=False)  72.3 us
    all_to_all x1, waiting for transfers between devices, narrow_scatter(): got = lax.all_to_all(blocks, 'narrow', 0, 0, tiled=False)  38.2 us
    all_to_all x1, starting transfers between devices, per_device(): lax.all_to_all(jnp.broadcast_to(attended[None], (count,) + attended.shape...  22 us
    all_to_all x2, starting transfers between devices, narrow_gather(): got = lax.all_to_all(slots, 'narrow', 0, 0, tiled=False)  18.5 us
    all_to_all x1, waiting for transfers between devices, per_device(): lax.all_to_all(jnp.broadcast_to(attended[None], (count,) + attended.shape...  13.2 us
    unnamed x97, local copies, waits for them, and re-layouts  11.8 us
  transfers between devices with their start and end apart: 20, of which 14 were waited for; matrix products, arithmetic and copies ran while one was open for 11% of the time, Pallas kernels for 0%

profile of v1, /device:TPU:0, one launch (start us, length us, event | category | flops | bytes accessed | tf_op | source)
XLA Modules:
  0.0 423.8 jit_solution(6389337917812001330)
XLA Ops:
  8.4 3.1 broadcast_in_dim.34
  11.5 6.0 %all-to-all-start = ((bf16[8,320,1024]{2,1,0:T(8,128)(2,1)}), bf16[8,320,1024]{2,1,0:T(8,128)(2,1)}, u32[]{:S(2)}, u32[]{:S(2)}) async-start(bf16[8,320,1024]{2,1,0:T(8,128)(2,1)} %broadcast_in_dim.34), calls=%async_computation | async-start | bytes 10485760 | tf_op jit(solution)/shard_map/all_to_all | solution.py:75
  19.2 59.1 %all-to-all-done = bf16[8,320,1024]{2,1,0:T(8,128)(2,1)} async-done(((bf16[8,320,1024]{2,1,0:T(8,128)(2,1)}), bf16[8,320,1024]{2,1,0:T(8,128)(2,1)}, u32[]{:S(2)}, u32[]{:S(2)}) %all-to-all-start) | async-done | bytes 5242912 | tf_op jit(solution)/shard_map/all_to_all | solution.py:75
  89.1 4.0 fusion.63
  97.6 22.0 %all-to-all-start.1 = ((bf16[8,768,128]{2,1,0:T(8,128)(2,1)}), bf16[8,768,128]{2,1,0:T(8,128)(2,1)S(1)}, u32[]{:S(2)}, u32[]{:S(2)}) async-start(bf16[8,768,128]{2,1,0:T(8,128)(2,1)} %broadcast_in_dim.39), calls=%async_computation.1 | async-start | bytes 3145728 | tf_op jit(solution)/shard_map/all_to_all | solution.py:253
  119.6 3.5 fusion.59
  126.4 13.2 %all-to-all-done.1 = bf16[8,768,128]{2,1,0:T(8,128)(2,1)S(1)} async-done(((bf16[8,768,128]{2,1,0:T(8,128)(2,1)}), bf16[8,768,128]{2,1,0:T(8,128)(2,1)S(1)}, u32[]{:S(2)}, u32[]{:S(2)}) %all-to-all-start.1) | async-done | bytes 1572896 | tf_op jit(solution)/shard_map/all_to_all | solution.py:253
  139.7 3.9 fusion.64
  156.1 4.4 %all-to-all-start.2 = ((bf16[8,96,2048]{2,1,0:T(8,128)(2,1)}), bf16[8,96,2048]{2,1,0:T(8,128)(2,1)}, u32[]{:S(2)}, u32[]{:S(2)}) async-start(bf16[8,96,2048]{2,1,0:T(8,128)(2,1)} %bitcast.81), calls=%async_computation.2 | async-start | bytes 6291456 | tf_op jit(solution)/shard_map/all_to_all | solution.py:81
  160.7 38.2 %all-to-all-done.2 = bf16[8,96,2048]{2,1,0:T(8,128)(2,1)} async-done(((bf16[8,96,2048]{2,1,0:T(8,128)(2,1)}), bf16[8,96,2048]{2,1,0:T(8,128)(2,1)}, u32[]{:S(2)}, u32[]{:S(2)}) %all-to-all-start.2) | async-done | bytes 3145760 | tf_op jit(solution)/shard_map/all_to_all | solution.py:81
  206.1 12.4 %all-to-all-start.3 = ((bf16[8,96,1024]{2,1,0:T(8,128)(2,1)}), bf16[8,96,1024]{2,1,0:T(8,128)(2,1)S(1)}, u32[]{:S(2)}, u32[]{:S(2)}) async-start(bf16[8,96,1024]{2,1,0:T(8,128)(2,1)} %broadcast_in_dim.40), calls=%async_computation.3 | async-start | bytes 3145728 | tf_op jit(solution)/shard_map/all_to_all | solution.py:75
  225.6 13.1 %all-to-all-done.3 = bf16[8,96,1024]{2,1,0:T(8,128)(2,1)S(1)} async-done(((bf16[8,96,1024]{2,1,0:T(8,128)(2,1)}), bf16[8,96,1024]{2,1,0:T(8,128)(2,1)S(1)}, u32[]{:S(2)}, u32[]{:S(2)}) %all-to-all-start.3) | async-done | bytes 1572896 | tf_op jit(solution)/shard_map/all_to_all | solution.py:75
  239.5 3.3 multiply_reduce_fusion
  261.1 4.7 %collective-permute-done.2 = bf16[128,512]{0,1:T(8,128)(2,1)S(1)} collective-permute-done((bf16[128,512]{0,1:T(8,128)(2,1)S(1)}, bf16[128,512]{0,1:T(8,128)(2,1)S(1)}, u32[]{:S(2)}, u32[]{:S(2)}) %collective-permute-start.2) | collective-permute-done | bytes 131104 | tf_op jit(solution)/shard_map/ppermute | solution.py:139
  266.0 5.4 %collective-permute-start.4 = (bf16[64,512]{0,1:T(8,128)(2,1)S(1)}, bf16[64,512]{0,1:T(8,128)(2,1)S(1)}, u32[]{:S(2)}, u32[]{:S(2)}) collective-permute-start(bf16[64,512]{0,1:T(8,128)(2,1)S(1)} %dynamic-slice_convert_fusion), channel_id=1, source_target_pairs={{0,64},{8,72},{16,80},{24,88},{32,96},{40,104},{48,112},{56,120},{... | collective-permute-start | bytes 196616 | tf_op jit(solution)/shard_map/ppermute | solution.py:143
  271.3 4.1 collective-permute-done.4
  275.6 4.0 collective-permute-start.5
  280.0 4.0 collective-permute-done.5
  287.8 3.6 all-to-all-start.4
  292.5 6.3 %collective-permute-done.7 = bf16[128,512]{0,1:T(8,128)(2,1)S(1)} collective-permute-done((bf16[128,512]{0,1:T(8,128)(2,1)S(1)}, bf16[128,512]{0,1:T(8,128)(2,1)S(1)}, u32[]{:S(2)}, u32[]{:S(2)}) %collective-permute-start.7) | collective-permute-done | bytes 131104 | tf_op jit(solution)/shard_map/ppermute | solution.py:154
  299.3 84.1 %all-reduce.2.cloned.1.call-done = bf16[1536,1024]{1,0:T(8,128)(2,1)} async-done(((bf16[1536,1024]{1,0:T(8,128)(2,1)}), bf16[1536,1024]{1,0:T(8,128)(2,1)}) %all-reduce.2.cloned.1.call-update) | async-done | bytes 3145744 | tf_op jit(solution)/shard_map/psum | solution.py:337
  383.5 2.9 slice.128
  401.8 3.7 collective-permute-done.11
  407.8 3.0 collective-permute-done.12
  (215 shorter events, 96.2 us)
Async XLA Ops:
  7.2 140.6 %copy-start = (bf16[1024,512]{1,0:T(8,128)(2,1)S(1)}, bf16[1024,512]{1,0:T(8,128)(2,1)}, u32[]{:S(2)}) copy-start(bf16[1024,512]{1,0:T(8,128)(2,1)} %param.22) | copy-start | bytes 3145732
  11.5 66.8 %all-to-all-start = ((bf16[8,320,1024]{2,1,0:T(8,128)(2,1)}), bf16[8,320,1024]{2,1,0:T(8,128)(2,1)}, u32[]{:S(2)}, u32[]{:S(2)}) async-start(bf16[8,320,1024]{2,1,0:T(8,128)(2,1)} %broadcast_in_dim.34), calls=%async_computation | async-start | bytes 10485760 | tf_op jit(solution)/shard_map/all_to_all | solution.py:75
  17.7 64.4 %copy-start.35 = (f32[1024]{0:T(1024)S(1)}, f32[1024]{0:T(1024)}, u32[]{:S(2)}) copy-start(f32[1024]{0:T(1024)} %param.24) | copy-start | bytes 12292
  17.7 64.4 %copy-start.37 = (f32[1024]{0:T(1024)S(1)}, f32[1024]{0:T(1024)}, u32[]{:S(2)}) copy-start(f32[1024]{0:T(1024)} %param.25) | copy-start | bytes 12292
  18.8 69.3 %copy-start.12 = (f32[768,32]{0,1:T(8,128)}, f32[768,32]{0,1:T(8,128)S(1)}, u32[]{:S(2)}) copy-start(f32[768,32]{0,1:T(8,128)S(1)} %get-tuple-element.87) | copy-start | bytes 294916
  97.6 42.1 %all-to-all-start.1 = ((bf16[8,768,128]{2,1,0:T(8,128)(2,1)}), bf16[8,768,128]{2,1,0:T(8,128)(2,1)S(1)}, u32[]{:S(2)}, u32[]{:S(2)}) async-start(bf16[8,768,128]{2,1,0:T(8,128)(2,1)} %broadcast_in_dim.39), calls=%async_computation.1 | async-start | bytes 3145728 | tf_op jit(solution)/shard_map/all_to_all | solution.py:253
  156.1 42.8 %all-to-all-start.2 = ((bf16[8,96,2048]{2,1,0:T(8,128)(2,1)}), bf16[8,96,2048]{2,1,0:T(8,128)(2,1)}, u32[]{:S(2)}, u32[]{:S(2)}) async-start(bf16[8,96,2048]{2,1,0:T(8,128)(2,1)} %bitcast.81), calls=%async_computation.2 | async-start | bytes 6291456 | tf_op jit(solution)/shard_map/all_to_all | solution.py:81
  206.1 32.6 %all-to-all-start.3 = ((bf16[8,96,1024]{2,1,0:T(8,128)(2,1)}), bf16[8,96,1024]{2,1,0:T(8,128)(2,1)S(1)}, u32[]{:S(2)}, u32[]{:S(2)}) async-start(bf16[8,96,1024]{2,1,0:T(8,128)(2,1)} %broadcast_in_dim.40), calls=%async_computation.3 | async-start | bytes 3145728 | tf_op jit(solution)/shard_map/all_to_all | solution.py:75
  218.6 164.9 %all-reduce.2.cloned.1.call-start = ((), (), s32[]{:S(2)}) async-start(), calls=%async_computation.5 | async-start | bytes 6291456 | tf_op jit(solution)/shard_map/psum | solution.py:337
  249.0 5.0 %collective-permute-start = (bf16[512,512]{0,1:T(8,128)(2,1)S(1)}, bf16[512,512]{0,1:T(8,128)(2,1)S(1)}, u32[]{:S(2)}, u32[]{:S(2)}) collective-permute-start(bf16[512,512]{0,1:T(8,128)(2,1)S(1)} %fusion.40), channel_id=1, source_target_pairs={{0,8},{8,0},{16,24},{24,16},{32,40},{40,32},{48,56},{56,48},{64,72... | collective-permute-start | bytes 1572872 | tf_op jit(solution)/shard_map/ppermute | solution.py:134
  254.3 6.8 %collective-permute-start.1 = (bf16[128,512]{0,1:T(8,128)(2,1)S(1)}, bf16[128,512]{0,1:T(8,128)(2,1)S(1)}, u32[]{:S(2)}, u32[]{:S(2)}) collective-permute-start(bf16[128,512]{0,1:T(8,128)(2,1)S(1)} %get-tuple-element.66), channel_id=1, source_target_pairs={{0,16},{8,24},{16,32},{24,40},{32,48},{40,56},{48,0},{56,8},{64,80... | collective-permute-start | bytes 393224 | tf_op jit(solution)/shard_map/ppermute | solution.py:139
  255.9 9.9 %collective-permute-start.2 = (bf16[128,512]{0,1:T(8,128)(2,1)S(1)}, bf16[128,512]{0,1:T(8,128)(2,1)S(1)}, u32[]{:S(2)}, u32[]{:S(2)}) collective-permute-start(bf16[128,512]{0,1:T(8,128)(2,1)S(1)} %get-tuple-element.68), channel_id=1, source_target_pairs={{0,32},{8,40},{16,48},{24,56},{32,0},{40,8},{48,16},{56,24},{64,96... | collective-permute-start | bytes 393224 | tf_op jit(solution)/shard_map/ppermute | solution.py:139
  258.6 7.2 %collective-permute-start.3 = (bf16[128,512]{0,1:T(8,128)(2,1)S(1)}, bf16[128,512]{0,1:T(8,128)(2,1)S(1)}, u32[]{:S(2)}, u32[]{:S(2)}) collective-permute-start(bf16[128,512]{0,1:T(8,128)(2,1)S(1)} %get-tuple-element.67), channel_id=1, source_target_pairs={{0,48},{8,56},{16,0},{24,8},{32,16},{40,24},{48,32},{56,40},{64,11... | collective-permute-start | bytes 393224 | tf_op jit(solution)/shard_map/ppermute | solution.py:139
  266.0 9.5 %collective-permute-start.4 = (bf16[64,512]{0,1:T(8,128)(2,1)S(1)}, bf16[64,512]{0,1:T(8,128)(2,1)S(1)}, u32[]{:S(2)}, u32[]{:S(2)}) collective-permute-start(bf16[64,512]{0,1:T(8,128)(2,1)S(1)} %dynamic-slice_convert_fusion), channel_id=1, source_target_pairs={{0,64},{8,72},{16,80},{24,88},{32,96},{40,104},{48,112},{56,120},{... | collective-permute-start | bytes 196616 | tf_op jit(solution)/shard_map/ppermute | solution.py:143
  275.6 8.4 %collective-permute-start.5 = (bf16[64,512]{0,1:T(8,128)(2,1)S(1)}, bf16[64,512]{0,1:T(8,128)(2,1)S(1)}, u32[]{:S(2)}, u32[]{:S(2)}) collective-permute-start(bf16[64,512]{0,1:T(8,128)(2,1)S(1)} %add_convert_fusion.5), channel_id=1, source_target_pairs={{0,64},{8,72},{16,80},{24,88},{32,96},{40,104},{48,112},{56,120},{... | collective-permute-start | bytes 196616 | tf_op jit(solution)/shard_map/ppermute | solution.py:148
  284.9 7.6 %collective-permute-start.6 = (bf16[128,512]{0,1:T(8,128)(2,1)S(1)}, bf16[128,512]{0,1:T(8,128)(2,1)S(1)}, u32[]{:S(2)}, u32[]{:S(2)}) collective-permute-start(bf16[128,512]{0,1:T(8,128)(2,1)S(1)} %dynamic_update_slice.25), channel_id=1, source_target_pairs={{0,48},{8,56},{16,0},{24,8},{32,16},{40,24},{48,32},{56,40},{64,11... | collective-permute-start | bytes 393224 | tf_op jit(solution)/shard_map/ppermute | solution.py:154
  287.8 112.3 %all-to-all-start.4 = ((bf16[8,112,1024]{2,1,0:T(8,128)(2,1)}), bf16[8,112,1024]{2,1,0:T(8,128)(2,1)S(1)}, u32[]{:S(2)}, u32[]{:S(2)}) async-start(bf16[8,112,1024]{2,1,0:T(8,128)(2,1)} %pad_maximum_fusion.2), calls=%async_computation.4 | async-start | bytes 3670016 | tf_op jit(solution)/shard_map/all_to_all | solution.py:334
  291.4 7.4 %collective-permute-start.7 = (bf16[128,512]{0,1:T(8,128)(2,1)S(1)}, bf16[128,512]{0,1:T(8,128)(2,1)S(1)}, u32[]{:S(2)}, u32[]{:S(2)}) collective-permute-start(bf16[128,512]{0,1:T(8,128)(2,1)S(1)} %dynamic_update_slice.25), channel_id=1, source_target_pairs={{0,32},{8,40},{16,48},{24,56},{32,0},{40,8},{48,16},{56,24},{64,96... | collective-permute-start | bytes 393224 | tf_op jit(solution)/shard_map/ppermute | solution.py:154
  291.5 7.7 %collective-permute-start.8 = (bf16[128,512]{0,1:T(8,128)(2,1)S(1)}, bf16[128,512]{0,1:T(8,128)(2,1)S(1)}, u32[]{:S(2)}, u32[]{:S(2)}) collective-permute-start(bf16[128,512]{0,1:T(8,128)(2,1)S(1)} %dynamic_update_slice.25), channel_id=1, source_target_pairs={{0,16},{8,24},{16,32},{24,40},{32,48},{40,56},{48,0},{56,8},{64,80... | collective-permute-start | bytes 393224 | tf_op jit(solution)/shard_map/ppermute | solution.py:154
  299.2 90.0 %collective-permute-start.9 = (bf16[512,512]{0,1:T(8,128)(2,1)S(1)}, bf16[512,512]{0,1:T(8,128)(2,1)}, u32[]{:S(2)}, u32[]{:S(2)}) collective-permute-start(bf16[512,512]{0,1:T(8,128)(2,1)S(1)} %constant_dynamic-update-slice_fusion.2), channel_id=1, source_target_pairs={{0,8},{8,0},{16,24},{24,16},{32,40},{40,32},{48,56},{56,48},{64,72... | collective-permute-start | bytes 1572872 | tf_op jit(solution)/shard_map/ppermute | solution.py:162
  400.5 1.3 collective-permute-start.10
  401.7 3.8 collective-permute-start.11
  405.6 5.2 %collective-permute-start.12 = (f32[4,1024]{1,0:T(4,128)S(1)}, f32[4,1024]{1,0:T(4,128)S(1)}, u32[]{:S(2)}, u32[]{:S(2)}) collective-permute-start(f32[4,1024]{1,0:T(4,128)S(1)} %add.230), channel_id=1, source_target_pairs={{0,32},{8,40},{16,48},{24,56},{32,0},{40,8},{48,16},{56,24},{64,96... | collective-permute-start | bytes 49160 | tf_op jit(solution)/shard_map/ppermute | solution.py:172
  410.8 5.2 %collective-permute-start.13 = (f32[4,1024]{1,0:T(4,128)S(1)}, f32[4,1024]{1,0:T(4,128)S(1)}, u32[]{:S(2)}, u32[]{:S(2)}) collective-permute-start(f32[4,1024]{1,0:T(4,128)S(1)} %add.231), channel_id=1, source_target_pairs={{0,64},{8,72},{16,80},{24,88},{32,96},{40,104},{48,112},{56,120},{... | collective-permute-start | bytes 49160 | tf_op jit(solution)/shard_map/ppermute | solution.py:173
  (42 other events, 195.4 us)
Sparse Core Ops, SparseCore 0:
  225.7 157.6 all-reduce.1
